TPU v7x, 32 devices: a whole 2x2x4 slice. The times are simulated.
32 devices in a mesh: lon: 2 (over core), lat: 4 (over y, x), mem: 4 (over z).
Axes of the slice: x: 2, y: 2, z: 4, core: 2. Of those that a mesh axis runs over, the one named last changes fastest.
Arguments:
- ensemble: bfloat16 [80, 4, 4, 128, 512], P('mem', None, None, 'lon', 'lat'), may hold values from -6 to 6
- huber: float32 [4, 4, 128, 512], P(None, None, 'lon', 'lat'), may hold values from 0.1 to 1
- innovation: float32 [4, 4, 128, 512], P(None, None, 'lon', 'lat'), may hold values from -6 to 6
- sea_mask: int32 [32, 128], P('lon', 'lat'), may hold values 0 or 1
Outputs:
- control: float32 [80, 4, 32, 128], P('mem', None, 'lon', 'lat')
- gradient: float32 [80, 4, 32, 128], P('mem', None, 'lon', 'lat')
All inputs are finite; a program needn't handle non-finite values. No bound on the sum of `sea_mask` on one device may be relied on, other than what follows from the above.
Results may differ from a plain program's by a relative error of at most 0.013.
Values may be sent and summed in bfloat16 or wider, within the bound.
No kernel may reach another device: no remote copies, remote signals or barrier semaphores. Data moves between devices by JAX's collectives and lax.ppermute only.
A program may use at most 128 MiB of HBM per device.

v0:
```python
import math

import jax
import jax.numpy as jnp
from jax import lax
from jax.sharding import PartitionSpec as P

MEMBERS = 80
RATIO = 4
DSTEPS = 4
ITERS = 3


diffusion_rate = 0.2


def extended(cells, sides, width):
    for axis, dim in sides:
        count = lax.axis_size(axis)
        ends = count - 1
        head = lax.slice_in_dim(cells, 0, width, axis=dim)
        tail = lax.slice_in_dim(cells, cells.shape[dim] - width, cells.shape[dim], axis=dim)
        cells = jnp.concatenate(
            [
                lax.ppermute(tail, axis, [(i, (i + 1) % count) for i in range(ends)]),
                cells,
                lax.ppermute(head, axis, [((i + 1) % count, i) for i in range(ends)]),
            ],
            axis=dim,
        )
    return cells


def hat_table(rows, cols, row_shift, col_shift):
    fine_pos = (jnp.arange(rows, dtype=jnp.float32) - row_shift + 0.5) / RATIO - 0.5
    coarse_pos = jnp.arange(cols, dtype=jnp.float32) - col_shift
    return jnp.maximum(0.0, 1.0 - jnp.abs(coarse_pos[None, :] - fine_pos[:, None]))


def smooth_once(padded):
    inner = padded[:, :, 1:-1, 1:-1]
    beside = (
        padded[:, :, 2:, 1:-1]
        + padded[:, :, :-2, 1:-1]
        + padded[:, :, 1:-1, 2:]
        + padded[:, :, 1:-1, :-2]
    )
    return inner + diffusion_rate * (beside - 4.0 * inner)


def inside_cells(count, width, position, devices):
    first = position * count - width
    where = first + jnp.arange(count + 2 * width, dtype=jnp.int32)
    whole = count * devices
    return ((where >= 0) & (where < whole)).astype(jnp.float32)


def smooth_deep(field, width):
    padded = extended(field, (("lon", 2), ("lat", 3)), width)
    rows_in = inside_cells(field.shape[2], width, lax.axis_index("lon"), lax.axis_size("lon"))
    cols_in = inside_cells(field.shape[3], width, lax.axis_index("lat"), lax.axis_size("lat"))
    for step in range(DSTEPS):
        padded = smooth_once(padded)
        trim = step + 1
        row_keep = rows_in[trim : rows_in.shape[0] - trim]
        col_keep = cols_in[trim : cols_in.shape[0] - trim]
        padded = padded * row_keep[:, None] * col_keep[None, :]
    return padded


def local(ensemble, huber, innovation, sea_mask):
    scale = 1.0 / math.sqrt(MEMBERS - 1)
    keep = sea_mask.astype(jnp.float32)
    cells_x, cells_y = sea_mask.shape
    fine_cols, fine_rows = (ensemble.shape[3], ensemble.shape[4])
    forward_x = hat_table(fine_cols, cells_x + 2, 0, 1)
    forward_y = hat_table(fine_rows, cells_y + 2, 0, 1)
    back_x = hat_table(fine_cols + 4, cells_x, 2, 0)
    back_y = hat_table(fine_rows + 4, cells_y, 2, 0)

    def adjoint(misfit):
        spread = (
            jnp.einsum("mvlxy,vlxy->mlxy", ensemble, misfit, preferred_element_type=jnp.float32)
            * scale
        )
        padded = extended(spread, (("lon", 2), ("lat", 3)), 2)
        back = jnp.einsum(
            "xc,mlxy,yd->mlcd", back_x, padded, back_y, precision=lax.Precision.HIGHEST
        )
        back = smooth_deep(back, DSTEPS)
        return keep * back

    misfit_start = (huber * innovation).astype(jnp.bfloat16)
    gradient = -adjoint(misfit_start)
    control = jnp.zeros_like(gradient)
    for step in range(ITERS):
        shaped = keep * gradient
        hessian_padded = smooth_deep(shaped, DSTEPS + 1)
        fine = jnp.einsum(
            "xc,mlcd,yd->mlxy",
            forward_x,
            hessian_padded,
            forward_y,
            precision=lax.Precision.HIGHEST,
        ).astype(jnp.bfloat16)
        partial_sum = jnp.einsum(
            "mvlxy,mlxy->vlxy", ensemble, fine, preferred_element_type=jnp.float32
        )
        total = lax.psum(partial_sum, "mem")
        hessian_misfit = (huber * (total * scale)).astype(jnp.bfloat16)
        image = gradient + adjoint(hessian_misfit)
        squares, curvature = lax.psum(
            (jnp.sum(gradient * gradient), jnp.sum(gradient * image)), ("lon", "lat", "mem")
        )
        alpha = squares / curvature
        control = control - alpha * gradient
        gradient = gradient - alpha * image
    return (control, gradient)


def solution(mesh):
    placed = (
        P("mem", None, None, "lon", "lat"),
        P(None, None, "lon", "lat"),
        P(None, None, "lon", "lat"),
        P("lon", "lat"),
    )
    return jax.shard_map(
        local,
        mesh=mesh,
        in_specs=placed,
        out_specs=(P("mem", None, "lon", "lat"), P("mem", None, "lon", "lat")),
        check_vma=False,
    )
```

profile of v0, /device:TPU:0, one launch (start us, length us, event | category | flops | bytes accessed | tf_op | source)
XLA Modules:
  0.0 666.2 jit_solution(17996090135539417670)
XLA Ops:
  8.5 4.2 fusion.3
  31.3 5.4 collective-permute-start.2
  40.5 11.1 %fusion.7 = f32[20,4,132,16]{2,3,1,0:T(8,128)S(1)} fusion(f32[20,4,68,2]{2,3,1,0:T(2,128)S(1)} %copy.100, f32[20,4,68,128]{2,3,1,0:T(8,128)} %copy.99, f32[20,4,68,2]{2,3,1,0:T(2,128)S(1)} %copy.98, f32[68]{0:T(128)S(1)} %multiply_add_fusion.3), kind=kOutput, calls=%fused_computation.14 | convolution fusion | flops 139311872 | bytes 3548432 | tf_op jit(solution)/shard_map/xc,mlxy,yd->mlcd/dot_general | solution.py:87
  59.0 4.5 collective-permute-start.6
  67.9 4.4 collective-permute-done.7
  97.8 4.5 collective-permute-done.11
  117.4 37.6 %all-reduce.7.cloned.1.call-done = f32[4,4,64,128]{3,2,1,0:T(8,128)} async-done(((f32[4,4,64,128]{3,2,1,0:T(8,128)}), f32[4,4,64,128]{3,2,1,0:T(8,128)}) %all-reduce.7.cloned.1.call-update) | async-done | bytes 524304 | tf_op jit(solution)/shard_map/psum | solution.py:109
  156.1 4.2 fusion.4
  188.7 11.1 %fusion.13 = f32[20,4,132,16]{2,3,1,0:T(8,128)S(1)} fusion(f32[20,4,68,2]{2,3,1,0:T(2,128)S(1)} %copy.115, f32[20,4,68,128]{2,3,1,0:T(8,128)} %copy.114, f32[20,4,68,2]{2,3,1,0:T(2,128)S(1)} %copy.113, f32[68]{0:T(128)} %copy-done.22), kind=kOutput, calls=%fused_computation.20 | convolution fusion | flops 139311872 | bytes 3548432 | tf_op jit(solution)/shard_map/xc,mlxy,yd->mlcd/dot_general | solution.py:87
  216.8 5.2 collective-permute-done.19
  229.8 39.9 %all-reduce.2 = (f32[]{:T(128)}, f32[]{:T(128)}) all-reduce(f32[]{:T(128)} %get-tuple-element.7, f32[]{:T(128)} %get-tuple-element.6), channel_id=1, replica_groups=mesh['lon'=2,'lat'=4,'mem'=4] {'lon','lat','mem'}, use_global_device_ids=true, to_apply=%region_1.0 | all-reduce | flops 2 | bytes 16 | tf_op jit(solution)/shard_map/psum | solution.py:112
  281.3 4.9 collective-permute-start.22
  292.0 4.9 collective-permute-done.23
  311.9 37.1 %all-reduce.9.cloned.1.call-done = f32[4,4,64,128]{3,2,1,0:T(8,128)} async-done(((f32[4,4,64,128]{3,2,1,0:T(8,128)}), f32[4,4,64,128]{3,2,1,0:T(8,128)}) %all-reduce.9.cloned.1.call-update) | async-done | bytes 524304 | tf_op jit(solution)/shard_map/psum | solution.py:109
  350.1 4.2 fusion.5
  382.7 11.1 %fusion.19 = f32[20,4,132,16]{2,3,1,0:T(8,128)S(1)} fusion(f32[20,4,68,2]{2,3,1,0:T(2,128)S(1)} %copy.130, f32[20,4,68,128]{2,3,1,0:T(8,128)} %copy.129, f32[20,4,68,2]{2,3,1,0:T(2,128)S(1)} %copy.128, f32[68]{0:T(128)} %copy-done.22), kind=kOutput, calls=%fused_computation.26 | convolution fusion | flops 139311872 | bytes 3548432 | tf_op jit(solution)/shard_map/xc,mlxy,yd->mlcd/dot_general | solution.py:87
  410.6 5.1 collective-permute-done.31
  423.6 39.5 %all-reduce.1 = (f32[]{:T(128)}, f32[]{:T(128)}) all-reduce(f32[]{:T(128)} %get-tuple-element.5, f32[]{:T(128)} %get-tuple-element.4), channel_id=1, replica_groups=mesh['lon'=2,'lat'=4,'mem'=4] {'lon','lat','mem'}, use_global_device_ids=true, to_apply=%region_6.0 | all-reduce | flops 2 | bytes 16 | tf_op jit(solution)/shard_map/psum | solution.py:112
  474.7 4.9 collective-permute-start.34
  485.4 5.0 collective-permute-done.35
  505.1 37.3 %all-reduce.11.cloned.1.call-done = f32[4,4,64,128]{3,2,1,0:T(8,128)} async-done(((f32[4,4,64,128]{3,2,1,0:T(8,128)}), f32[4,4,64,128]{3,2,1,0:T(8,128)}) %all-reduce.11.cloned.1.call-update) | async-done | bytes 524304 | tf_op jit(solution)/shard_map/psum | solution.py:109
  576.3 11.1 %fusion.25 = f32[20,4,132,16]{2,3,1,0:T(8,128)S(1)} fusion(f32[20,4,68,2]{2,3,1,0:T(2,128)S(1)} %copy.145, f32[20,4,68,128]{2,3,1,0:T(8,128)} %copy.144, f32[20,4,68,2]{2,3,1,0:T(2,128)S(1)} %copy.143, f32[68]{0:T(128)} %copy-done.22), kind=kOutput, calls=%fused_computation.32 | convolution fusion | flops 139311872 | bytes 3548432 | tf_op jit(solution)/shard_map/xc,mlxy,yd->mlcd/dot_general | solution.py:87
  604.3 5.2 collective-permute-done.43
  617.3 39.5 %all-reduce = (f32[]{:T(128)}, f32[]{:T(128)}) all-reduce(f32[]{:T(128)} %get-tuple-element.3, f32[]{:T(128)} %get-tuple-element.2), channel_id=1, replica_groups=mesh['lon'=2,'lat'=4,'mem'=4] {'lon','lat','mem'}, use_global_device_ids=true, to_apply=%region_11.0 | all-reduce | flops 2 | bytes 16 | tf_op jit(solution)/shard_map/psum | solution.py:112
  (385 shorter events, 304.2 us)
Async XLA Ops:
  7.2 147.8 %all-reduce.7.cloned.1.call-start = ((), (), s32[]{:S(2)}) async-start(), calls=%async_computation | async-start | bytes 1048576 | tf_op jit(solution)/shard_map/psum | solution.py:109
  27.6 12.7 %collective-permute-start.3 = (f32[20,4,68,2]{2,1,3,0:T(4,128)S(1)}, f32[20,4,68,2]{2,1,3,0:T(4,128)S(1)}, u32[]{:S(2)}, u32[]{:S(2)}) collective-permute-start(f32[20,4,68,2]{2,1,3,0:T(4,128)S(1)} %copy.214), channel_id=1, source_target_pairs={{4,0},{8,4},{12,8},{5,1},{9,5},{13,9},{6,2},{10,6},{14,10},{7,3},{... | collective-permute-start | bytes 130568 | tf_op jit(solution)/shard_map/ppermute | solution.py:27
  31.3 9.1 %collective-permute-start.2 = (f32[20,4,68,2]{2,1,3,0:T(4,128)S(1)}, f32[20,4,68,2]{2,1,3,0:T(4,128)S(1)}, u32[]{:S(2)}, u32[]{:S(2)}) collective-permute-start(f32[20,4,68,2]{2,1,3,0:T(4,128)S(1)} %copy.213), channel_id=1, source_target_pairs={{0,4},{4,8},{8,12},{1,5},{5,9},{9,13},{2,6},{6,10},{10,14},{3,7},{... | collective-permute-start | bytes 130568 | tf_op jit(solution)/shard_map/ppermute | solution.py:25
  59.0 8.3 %collective-permute-start.6 = (f32[20,4,24,4]{2,3,1,0:T(4,128)S(1)}, f32[20,4,24,4]{2,3,1,0:T(4,128)S(1)}, u32[]{:S(2)}, u32[]{:S(2)}) collective-permute-start(f32[20,4,24,4]{2,3,1,0:T(4,128)S(1)} %copy.101), channel_id=1, source_target_pairs={{0,4},{4,8},{8,12},{1,5},{5,9},{9,13},{2,6},{6,10},{10,14},{3,7},{... | collective-permute-start | bytes 92168 | tf_op jit(solution)/shard_map/ppermute | solution.py:25
  64.2 8.1 %collective-permute-start.7 = (f32[20,4,24,4]{2,3,1,0:T(4,128)S(1)}, f32[20,4,24,4]{2,3,1,0:T(4,128)}, u32[]{:S(2)}, u32[]{:S(2)}) collective-permute-start(f32[20,4,24,4]{2,3,1,0:T(4,128)S(1)} %copy.102), channel_id=1, source_target_pairs={{4,0},{8,4},{12,8},{5,1},{9,5},{13,9},{6,2},{10,6},{14,10},{7,3},{... | collective-permute-start | bytes 92168 | tf_op jit(solution)/shard_map/ppermute | solution.py:27
  87.9 8.4 %collective-permute-start.10 = (f32[20,4,26,5]{2,1,3,0:T(4,128)}, f32[20,4,26,5]{2,1,3,0:T(4,128)}, u32[]{:S(2)}, u32[]{:S(2)}) collective-permute-start(f32[20,4,26,5]{2,1,3,0:T(4,128)} %copy.105), channel_id=1, source_target_pairs={{0,4},{4,8},{8,12},{1,5},{5,9},{9,13},{2,6},{6,10},{10,14},{3,7},{... | collective-permute-start | bytes 124808 | tf_op jit(solution)/shard_map/ppermute | solution.py:25
  93.3 9.0 %collective-permute-start.11 = (f32[20,4,26,5]{2,1,3,0:T(4,128)}, f32[20,4,26,5]{2,1,3,0:T(4,128)}, u32[]{:S(2)}, u32[]{:S(2)}) collective-permute-start(f32[20,4,26,5]{2,1,3,0:T(4,128)} %copy.106), channel_id=1, source_target_pairs={{4,0},{8,4},{12,8},{5,1},{9,5},{13,9},{6,2},{10,6},{14,10},{7,3},{... | collective-permute-start | bytes 124808 | tf_op jit(solution)/shard_map/ppermute | solution.py:27
  117.0 232.0 %all-reduce.9.cloned.1.call-start = ((), (), s32[]{:S(2)}) async-start(), calls=%async_computation.1 | async-start | bytes 1048576 | tf_op jit(solution)/shard_map/psum | solution.py:109
  174.1 12.1 %collective-permute-start.14 = (f32[20,4,68,2]{2,1,3,0:T(4,128)S(1)}, f32[20,4,68,2]{2,1,3,0:T(4,128)}, u32[]{:S(2)}, u32[]{:S(2)}) collective-permute-start(f32[20,4,68,2]{2,1,3,0:T(4,128)S(1)} %copy.215), channel_id=1, source_target_pairs={{0,4},{4,8},{8,12},{1,5},{5,9},{9,13},{2,6},{6,10},{10,14},{3,7},{... | collective-permute-start | bytes 130568 | tf_op jit(solution)/shard_map/ppermute | solution.py:25
  181.1 6.6 collective-permute-start.15
  208.1 8.2 %collective-permute-start.18 = (f32[20,4,24,4]{2,3,1,0:T(4,128)}, f32[20,4,24,4]{2,3,1,0:T(4,128)S(1)}, u32[]{:S(2)}, u32[]{:S(2)}) collective-permute-start(f32[20,4,24,4]{2,3,1,0:T(4,128)} %copy.116), channel_id=1, source_target_pairs={{0,4},{4,8},{8,12},{1,5},{5,9},{9,13},{2,6},{6,10},{10,14},{3,7},{... | collective-permute-start | bytes 92168 | tf_op jit(solution)/shard_map/ppermute | solution.py:25
  212.8 9.2 %collective-permute-start.19 = (f32[20,4,24,4]{2,3,1,0:T(4,128)S(1)}, f32[20,4,24,4]{2,3,1,0:T(4,128)}, u32[]{:S(2)}, u32[]{:S(2)}) collective-permute-start(f32[20,4,24,4]{2,3,1,0:T(4,128)S(1)} %copy.117), channel_id=1, source_target_pairs={{4,0},{8,4},{12,8},{5,1},{9,5},{13,9},{6,2},{10,6},{14,10},{7,3},{... | collective-permute-start | bytes 92168 | tf_op jit(solution)/shard_map/ppermute | solution.py:27
  281.3 9.1 %collective-permute-start.22 = (f32[20,4,26,5]{2,1,3,0:T(4,128)}, f32[20,4,26,5]{2,1,3,0:T(4,128)}, u32[]{:S(2)}, u32[]{:S(2)}) collective-permute-start(f32[20,4,26,5]{2,1,3,0:T(4,128)} %copy.120), channel_id=1, source_target_pairs={{0,4},{4,8},{8,12},{1,5},{5,9},{9,13},{2,6},{6,10},{10,14},{3,7},{... | collective-permute-start | bytes 124808 | tf_op jit(solution)/shard_map/ppermute | solution.py:25
  287.5 9.5 %collective-permute-start.23 = (f32[20,4,26,5]{2,1,3,0:T(4,128)}, f32[20,4,26,5]{2,1,3,0:T(4,128)}, u32[]{:S(2)}, u32[]{:S(2)}) collective-permute-start(f32[20,4,26,5]{2,1,3,0:T(4,128)} %copy.121), channel_id=1, source_target_pairs={{4,0},{8,4},{12,8},{5,1},{9,5},{13,9},{6,2},{10,6},{14,10},{7,3},{... | collective-permute-start | bytes 124808 | tf_op jit(solution)/shard_map/ppermute | solution.py:27
  311.6 230.8 %all-reduce.11.cloned.1.call-start = ((), (), s32[]{:S(2)}) async-start(), calls=%async_computation.2 | async-start | bytes 1048576 | tf_op jit(solution)/shard_map/psum | solution.py:109
  368.0 11.9 %collective-permute-start.26 = (f32[20,4,68,2]{2,1,3,0:T(4,128)S(1)}, f32[20,4,68,2]{2,1,3,0:T(4,128)}, u32[]{:S(2)}, u32[]{:S(2)}) collective-permute-start(f32[20,4,68,2]{2,1,3,0:T(4,128)S(1)} %copy.217), channel_id=1, source_target_pairs={{0,4},{4,8},{8,12},{1,5},{5,9},{9,13},{2,6},{6,10},{10,14},{3,7},{... | collective-permute-start | bytes 130568 | tf_op jit(solution)/shard_map/ppermute | solution.py:25
  375.1 6.6 collective-permute-start.27
  402.0 8.0 %collective-permute-start.30 = (f32[20,4,24,4]{2,3,1,0:T(4,128)}, f32[20,4,24,4]{2,3,1,0:T(4,128)S(1)}, u32[]{:S(2)}, u32[]{:S(2)}) collective-permute-start(f32[20,4,24,4]{2,3,1,0:T(4,128)} %copy.131), channel_id=1, source_target_pairs={{0,4},{4,8},{8,12},{1,5},{5,9},{9,13},{2,6},{6,10},{10,14},{3,7},{... | collective-permute-start | bytes 92168 | tf_op jit(solution)/shard_map/ppermute | solution.py:25
  406.6 9.2 %collective-permute-start.31 = (f32[20,4,24,4]{2,3,1,0:T(4,128)S(1)}, f32[20,4,24,4]{2,3,1,0:T(4,128)}, u32[]{:S(2)}, u32[]{:S(2)}) collective-permute-start(f32[20,4,24,4]{2,3,1,0:T(4,128)S(1)} %copy.132), channel_id=1, source_target_pairs={{4,0},{8,4},{12,8},{5,1},{9,5},{13,9},{6,2},{10,6},{14,10},{7,3},{... | collective-permute-start | bytes 92168 | tf_op jit(solution)/shard_map/ppermute | solution.py:27
  474.7 9.1 %collective-permute-start.34 = (f32[20,4,26,5]{2,1,3,0:T(4,128)}, f32[20,4,26,5]{2,1,3,0:T(4,128)}, u32[]{:S(2)}, u32[]{:S(2)}) collective-permute-start(f32[20,4,26,5]{2,1,3,0:T(4,128)} %copy.135), channel_id=1, source_target_pairs={{0,4},{4,8},{8,12},{1,5},{5,9},{9,13},{2,6},{6,10},{10,14},{3,7},{... | collective-permute-start | bytes 124808 | tf_op jit(solution)/shard_map/ppermute | solution.py:25
  480.9 9.5 %collective-permute-start.35 = (f32[20,4,26,5]{2,1,3,0:T(4,128)}, f32[20,4,26,5]{2,1,3,0:T(4,128)}, u32[]{:S(2)}, u32[]{:S(2)}) collective-permute-start(f32[20,4,26,5]{2,1,3,0:T(4,128)} %copy.136), channel_id=1, source_target_pairs={{4,0},{8,4},{12,8},{5,1},{9,5},{13,9},{6,2},{10,6},{14,10},{7,3},{... | collective-permute-start | bytes 124808 | tf_op jit(solution)/shard_map/ppermute | solution.py:27
  561.7 12.0 %collective-permute-start.38 = (f32[20,4,68,2]{2,1,3,0:T(4,128)S(1)}, f32[20,4,68,2]{2,1,3,0:T(4,128)}, u32[]{:S(2)}, u32[]{:S(2)}) collective-permute-start(f32[20,4,68,2]{2,1,3,0:T(4,128)S(1)} %copy.219), channel_id=1, source_target_pairs={{0,4},{4,8},{8,12},{1,5},{5,9},{9,13},{2,6},{6,10},{10,14},{3,7},{... | collective-permute-start | bytes 130568 | tf_op jit(solution)/shard_map/ppermute | solution.py:25
  595.7 8.0 %collective-permute-start.42 = (f32[20,4,24,4]{2,3,1,0:T(4,128)}, f32[20,4,24,4]{2,3,1,0:T(4,128)S(1)}, u32[]{:S(2)}, u32[]{:S(2)}) collective-permute-start(f32[20,4,24,4]{2,3,1,0:T(4,128)} %copy.146), channel_id=1, source_target_pairs={{0,4},{4,8},{8,12},{1,5},{5,9},{9,13},{2,6},{6,10},{10,14},{3,7},{... | collective-permute-start | bytes 92168 | tf_op jit(solution)/shard_map/ppermute | solution.py:25
  600.2 9.2 %collective-permute-start.43 = (f32[20,4,24,4]{2,3,1,0:T(4,128)S(1)}, f32[20,4,24,4]{2,3,1,0:T(4,128)}, u32[]{:S(2)}, u32[]{:S(2)}) collective-permute-start(f32[20,4,24,4]{2,3,1,0:T(4,128)S(1)} %copy.147), channel_id=1, source_target_pairs={{4,0},{8,4},{12,8},{5,1},{9,5},{13,9},{6,2},{10,6},{14,10},{7,3},{... | collective-permute-start | bytes 92168 | tf_op jit(solution)/shard_map/ppermute | solution.py:27
  (88 other events, 874.8 us)
Sparse Core Ops, SparseCore 0:
  117.1 37.8 all-reduce.6
  311.8 37.1 all-reduce.8
  505.3 37.1 all-reduce.10
where the time goes:
time: 674 us; the launch traced here: 666 us
  waiting for transfers between devices  182 us (27%)
  blocking collectives  119 us (18%)
  local copies, waits for them, and re-layouts  113 us (17%)
  starting transfers between devices  94.1 us (14%)
  other arithmetic  76.6 us (11%)
  matrix products  61.5 us (9%)
  between operations  20 us (3%)
    psum x3, blocking collectives, local(): lax.psum((jnp.sum(gradient * gradient), jnp.sum(gradient * image)), ('lon...  119 us
    psum x3, waiting for transfers between devices, local(): total = lax.psum(partial_sum, 'mem')  112 us
    ppermute x22, starting transfers between devices, extended(): lax.ppermute(tail, axis, [(i, (i + 1) % count) for i in range(ends)])  63.9 us
    ppermute x22, waiting for transfers between devices, extended(): lax.ppermute(head, axis, [((i + 1) % count, i) for i in range(ends)])  58.4 us
    dot_general x8, matrix products, adjoint(): jnp.einsum('xc,mlxy,yd->mlcd', back_x, padded, back_y, precision=lax.Prec...  49.3 us
    slice x29, local copies, waits for them, and re-layouts, extended(): lax.slice_in_dim(cells, cells.shape[dim] - width, cells.shape[dim], axis=...  34.3 us
    unnamed x142, local copies, waits for them, and re-layouts  31.1 us
    ppermute x22, starting transfers between devices, extended(): lax.ppermute(head, axis, [((i + 1) % count, i) for i in range(ends)])  29.5 us
  transfers between devices with their start and end apart: 47, of which 31 were waited for; matrix products, arithmetic and copies ran while one was open for 6% of the time, Pallas kernels for 0%

commit v1 on v0

v1 whole, which is shorter than its diff:
```python
import math

import jax
import jax.numpy as jnp
import numpy as np
from jax import lax
from jax.experimental import pallas as pl
from jax.experimental.pallas import tpu as pltpu
from jax.sharding import PartitionSpec as P

MEMBERS = 80
DSTEPS = 4
ITERS = 3
RATE = 0.2
LANES = 128
HALO = DSTEPS + 1
STRIP = 2 * HALO
PACK = STRIP + HALO
TERMS = DSTEPS + 1
F32 = jnp.float32
BF16 = jnp.bfloat16


def hat_table(rows, cols, col_shift, ratio):
    fine = (np.arange(rows) + 0.5) / ratio - 0.5
    coarse = np.arange(cols) - col_shift
    return np.maximum(0.0, 1.0 - np.abs(coarse[None, :] - fine[:, None]))


def axis_terms(cells, fine, devices, powers):
    ext = cells + 2 * HALO
    hat = hat_table(fine, ext, HALO, fine // cells)
    out = []
    for at in range(devices):
        where = at * cells - HALO + np.arange(ext)
        inside = ((where >= 0) & (where < cells * devices)).astype(np.float64)
        step = (0.5 - 2 * RATE) * np.eye(ext) + RATE * (np.eye(ext, k=1) + np.eye(ext, k=-1))
        step = inside[:, None] * step * inside[None, :]
        out.append([hat @ (np.diag(inside) @ np.linalg.matrix_power(step, p)) for p in powers])
    return np.array(out)


def thirds(value):
    hi = value.astype(BF16).astype(F32)
    mid = (value - hi).astype(BF16).astype(F32)
    return hi, mid, value - hi - mid


def iota(shape, axis):
    return lax.broadcasted_iota(jnp.int32, shape, axis)


def rows_of(shape, first, values):
    at = iota(shape, 0)
    out = jnp.zeros(shape, F32)
    for k, v in enumerate(values):
        out = jnp.where(at == first + k, v, out)
    return out


def build(mesh_shape, ens_shape, mask_shape):
    members, nvar, levels, fx, fy = ens_shape
    cx, cy = mask_shape
    n_lon, n_lat, n_mem = (mesh_shape[a] for a in ("lon", "lat", "mem"))
    scale = 1.0 / math.sqrt(MEMBERS - 1)
    ex, ey = cx + 2 * HALO, cy + 2 * HALO
    exp = cx + 16
    assert levels == n_mem and fy == LANES and exp >= ex + 6 and exp % 16 == 0 and members % 2 == 0
    assert cx >= STRIP and cy >= STRIP and ey <= 48 and fx % 16 == 0
    fields = levels * members

    def packing(width):
        groups = next(g for g in range(1, fields + 1) if fields % g == 0 and (fields // g) * width <= LANES)
        return groups, fields // groups

    krows = TERMS * exp
    klanes = TERMS * LANES

    coef = [math.comb(DSTEPS, k) for k in range(TERMS)]
    ax = axis_terms(cx, fx, n_lon, range(TERMS))
    by = axis_terms(cy, fy, n_lat, [DSTEPS - k for k in range(TERMS)])
    a_np = np.zeros((n_lon, fx, TERMS, exp))
    a_np[..., :ex] = np.moveaxis(ax, 1, 2) * np.array(coef)[None, None, :, None]
    a_np = a_np.reshape(n_lon, fx, krows)
    b_np = np.zeros((n_lat, TERMS, fy, LANES))
    b_np[..., :ey] = by
    b_np = b_np.reshape(n_lat, klanes, LANES)
    def halves(table):
        hi = table.astype(BF16).astype(np.float64)
        return hi, table - hi

    a_tab = jnp.asarray(a_np, BF16)
    at_tab = jnp.asarray(np.concatenate(halves(np.swapaxes(a_np, 1, 2)), axis=2), BF16)
    b_hi, b_lo = halves(b_np)
    b_both = b_hi + np.roll(b_lo, 64, axis=2)
    bn_tab = jnp.asarray(b_both, BF16)
    bt_tab = jnp.asarray(np.swapaxes(b_both, 1, 2), BF16)

    prows = nvar * fx
    chunks = fx // 16
    sds = jax.ShapeDtypeStruct
    vmem = pl.BlockSpec(memory_space=pltpu.VMEM)
    smem = pl.BlockSpec(memory_space=pltpu.SMEM)

    def level(j, ix):
        return lax.rem(ix[0] + j, levels)

    def call(body, name, ins, shapes, scratch=()):
        return pl.pallas_call(
            body,
            name=name,
            in_specs=[smem] + [vmem] * ins,
            out_specs=[vmem] * len(shapes),
            out_shape=shapes,
            scratch_shapes=scratch,
            compiler_params=pltpu.CompilerParams(vmem_limit_bytes=16 << 20),
        )

    payload = sds((prows + 16, fy), BF16)
    small = sds((8, LANES), F32)

    def forward(d):
        def body(ix, ens, g, keep, a, bt, gg, out, t, w):
            lev = level(d, ix)
            field = g[d * members : (d + 1) * members] * keep[...][None]
            field = (field + pltpu.roll(field, 64, 2)).reshape(members * exp, LANES).astype(BF16)
            t[...] = jnp.dot(field, bt[ix[2]], preferred_element_type=F32).astype(BF16)
            for m in range(0, members, 2):
                rhs = jnp.concatenate(
                    [
                        jnp.concatenate(
                            [t[(m + i) * exp : (m + i + 1) * exp, k * LANES : (k + 1) * LANES] for i in range(2)],
                            axis=1,
                        )
                        for k in range(TERMS)
                    ],
                    axis=0,
                )
                pair = jnp.dot(a[ix[1]], rhs, preferred_element_type=F32)
                w[m] = pair[:, :LANES].astype(BF16)
                w[m + 1] = pair[:, LANES:].astype(BF16)

            def chunk(c, carry):
                at = pl.multiple_of(c * 16, 16)
                acc = jnp.zeros((nvar, 16, fy), F32)
                for m in range(members):
                    acc = acc + ens[m, :, lev, pl.ds(at, 16), :].astype(F32) * w[m, pl.ds(at, 16), :].astype(F32)[None]
                for v in range(nvar):
                    out[pl.ds(pl.multiple_of(v * fx + at, 16), 16), :] = acc[v].astype(BF16)
                return carry

            lax.fori_loop(0, chunks, chunk, 0)
            out[pl.ds(prows, 16), :] = rows_of((16, LANES), 0, thirds(gg[0:1, :])).astype(BF16)

        scratch = [pltpu.VMEM((members * exp, klanes), BF16), pltpu.VMEM((members, fx, fy), BF16)]
        return call(body, f"forward{d}", 6, [payload], scratch)

    def misfit_body(ix, huber, *rest):
        parts, (out, gg) = rest[:levels], rest[levels:]
        total = parts[0][...].astype(F32)
        for p in parts[1:]:
            total = total + p[...].astype(F32)
        weight = huber[:, ix[0]].reshape(prows, fy)
        out[...] = (weight * (total[:prows] * scale)).astype(BF16)
        tail = total[prows:]
        gg[...] = jnp.broadcast_to(tail[0:1] + tail[1:2] + tail[2:3], (8, LANES))

    misfit_own = call(misfit_body, "misfit", 1 + levels, [sds((prows, fy), BF16), small])

    def adjoint_core(ens, lev, mis, at, bn, sp, zs):
        def chunk(c, carry):
            row = pl.multiple_of(c * 16, 16)
            mv = [mis[pl.ds(pl.multiple_of(v * fx + row, 16), 16), :].astype(F32) for v in range(nvar)]
            for m in range(members):
                s = ens[m, 0, lev, pl.ds(row, 16), :].astype(F32) * mv[0]
                for v in range(1, nvar):
                    s = s + ens[m, v, lev, pl.ds(row, 16), :].astype(F32) * mv[v]
                s = s.astype(BF16)
                sp[pl.ds(row, 16), pl.ds(m * LANES, LANES)] = s
                sp[pl.ds(pl.multiple_of(fx + row, 16), 16), pl.ds(m * LANES, LANES)] = s
            return carry

        lax.fori_loop(0, chunks, chunk, 0)
        for m in range(0, members, 2):
            z = jnp.dot(at, sp[:, m * LANES : (m + 2) * LANES], preferred_element_type=F32).astype(BF16)
            for i in range(2):
                for k in range(TERMS):
                    zs[(m + i) * exp : (m + i + 1) * exp, k * LANES : (k + 1) * LANES] = z[
                        k * exp : (k + 1) * exp, i * LANES : (i + 1) * LANES
                    ]
        both = jnp.dot(zs[...], bn, preferred_element_type=F32) * scale
        lane = iota((1, LANES), 1)
        res = jnp.where(lane < 64, both + pltpu.roll(both, 64, 1), 0.0)
        return res.reshape(members, exp, LANES)

    n_strips = 1 if n_lon == 2 else 2

    def strips_of(lon, block, tail):
        lo, hi = block[:, :16], block[:, cx : cx + 16]
        sends = [jnp.where(lon == 0, hi, lo)] if n_lon == 2 else [hi, lo]
        row = iota((1, 16, 1), 1) < STRIP
        return [jnp.where(row, s, tail[None]) for s in sends]

    part_shape = sds((members, exp, LANES), F32)

    strip_shape = sds((fields, 16, LANES), F32)

    adj_scratch = [
        pltpu.VMEM((2 * fx, members * LANES), BF16),
        pltpu.VMEM((members * exp, klanes), BF16),
    ]

    def first_body(ix, ens, huber, innov, at, bn, extra, q, *rest):
        strips, (mis, sp, zs) = rest[:n_strips], rest[n_strips:]
        j = pl.program_id(0)
        mis[...] = (huber[:, 0] * innov[:, 0]).astype(BF16).reshape(prows, fy)
        res = adjoint_core(ens, 0, mis, at[0], bn[0], sp, zs)
        here = (iota((members, 1, 1), 0) == 0) & (j == 0)
        res = res + jnp.where(here, extra[...][None], 0.0)
        q[0] = res
        for ref, val in zip(strips, strips_of(ix[1], res, jnp.zeros((16, LANES), F32))):
            ref[...] = val

    def table(arr, slot):
        return pl.BlockSpec((1,) + arr.shape[1:], lambda j, ix: (ix[slot], 0, 0))

    obs_spec = pl.BlockSpec((nvar, 1, fx, fy), lambda j, ix: (0, level(j, ix), 0, 0))
    first_adjoint = pl.pallas_call(
        first_body,
        name="first_adjoint",
        out_shape=[sds((levels, members, exp, LANES), F32)] + [strip_shape] * n_strips,
        grid_spec=pltpu.PrefetchScalarGridSpec(
            num_scalar_prefetch=1,
            grid=(levels,),
            in_specs=[
                pl.BlockSpec((members, nvar, 1, fx, fy), lambda j, ix: (0, 0, level(j, ix), 0, 0)),
                obs_spec,
                obs_spec,
                table(at_tab, 1),
                table(bn_tab, 2),
                pl.BlockSpec((exp, LANES), lambda j, ix: (0, 0)),
            ],
            out_specs=[pl.BlockSpec((1, members, exp, LANES), lambda j, ix: (j, 0, 0, 0))]
            + [pl.BlockSpec((members, 16, LANES), lambda j, ix: (j, 0, 0))] * n_strips,
            scratch_shapes=[pltpu.VMEM((prows, fy), BF16)] + adj_scratch,
        ),
        compiler_params=pltpu.CompilerParams(vmem_limit_bytes=24 << 20),
    )

    def adjoint(d, others):
        def body(ix, ens, huber, at, bn, mis, *rest):
            final = others > 0
            if final:
                gg, rest = rest[0], rest[1:]
                qs, parts, rest = rest[:others], rest[others : 2 * others], rest[2 * others :]
            q, sums, rest = rest[0], rest[1], rest[2:]
            strips, (sp, zs) = rest[: n_strips * final], rest[n_strips * final :]
            lev = level(d, ix)
            value = mis[...].astype(F32)
            part = jnp.sum(value * value / huber[:, lev].reshape(prows, fy), axis=0, keepdims=True)
            part = jnp.broadcast_to(jnp.sum(part, axis=1, keepdims=True), (1, LANES))
            res = adjoint_core(ens, lev, mis, at[ix[1]], bn[ix[2]], sp, zs)
            q[...] = res
            if not final:
                sums[...] = jnp.broadcast_to(part, (8, LANES))
                return
            for p in parts:
                part = part + p[0:1]
            sums[...] = rows_of((8, LANES), 0, [gg[0:1, :], part])
            tail = rows_of((16, LANES), STRIP, [*thirds(gg[0:1, :]), *thirds(part)])
            for lvl, ref in [(order[i], qs[i]) for i in range(others)] + [(d, q)]:
                for out, val in zip(strips, strips_of(ix[1], ref[...], tail)):
                    out[lvl * members : (lvl + 1) * members] = val

        final = others > 0
        shapes = [part_shape, small] + [strip_shape] * (n_strips * final)
        return call(body, f"adjoint{d}", 5 + (1 + 2 * others) * final, shapes, adj_scratch)

    order = [0] + [d for d in (1, levels - 1) if d > 0 and d < levels]
    order = list(dict.fromkeys(order))
    order = order + [d for d in range(levels) if d not in order]

    full_q = (fields, exp, LANES)

    def masks(ix, slot, size):
        at = ix[slot]
        return (at > 0).astype(F32), (at < size - 1).astype(F32)

    def tail_sums(tail, row):
        t = [tail[row + k : row + k + 1].astype(F32) for k in range(6)]
        return t[0] + t[1] + t[2], t[3] + t[4] + t[5]

    def lon_join(first, last):
        kind = F32 if last else BF16
        width = HALO if last else PACK
        groups, packs = packing(width)
        src_hi = cy + HALO if last else cy

        def body(ix, *rest):
            if first:
                q_in, rest = [rest[0].at[d] for d in range(levels)], rest[1:]
            else:
                q_in, sc, rest = rest[:levels], rest[levels], rest[levels + 1 :]
            recv, (out, to_next, to_prev, *sums) = rest[:n_strips], rest[n_strips:]
            has_lo, has_hi = masks(ix, 1, n_lon)
            if not first:
                total = sc[...]
                for r in recv:
                    total = total + rows_of((8, LANES), 0, tail_sums(r[fields - 1], STRIP))
                sums[0][...] = total
            strip_rows = iota((1, 16, 1), 1) < STRIP

            def joined(mine, theirs, here):
                return jnp.where(strip_rows & (here > 0), mine + theirs, mine)

            for d in range(levels):
                at = slice(d * members, (d + 1) * members)
                q = q_in[d]
                out[at, 0:16, :] = joined(q[:, 0:16, :], recv[0][at], has_lo)
                for r0 in range(16, cx, 16):
                    out[at, r0 : r0 + 16, :] = q[:, r0 : r0 + 16, :]
                out[at, cx : cx + 16, :] = joined(q[:, cx : cx + 16, :], recv[-1][at], has_hi)
            lane = iota((1, 1, LANES), 2)
            nxt = jnp.zeros((groups, exp, LANES), F32)
            prv = jnp.zeros((groups, exp, LANES), F32)
            for p in range(packs):
                block = out[p * groups : (p + 1) * groups]
                at = p * width
                wide = HALO if last else STRIP
                here = (lane >= at) & (lane < at + wide)
                prv = jnp.where(here, pltpu.roll(block, at % LANES, 2), prv)
                nxt = jnp.where(here, pltpu.roll(block, (at - src_hi) % LANES, 2), nxt)
                if not last:
                    low = block - block.astype(BF16).astype(F32)
                    here = (lane >= at + STRIP) & (lane < at + PACK)
                    prv = jnp.where(here, pltpu.roll(low, (at + STRIP - HALO) % LANES, 2), prv)
                    nxt = jnp.where(here, pltpu.roll(low, (at + STRIP - cy) % LANES, 2), nxt)
            if first:
                to_next[0:groups] = nxt.astype(kind)
                to_prev[0:groups] = prv.astype(kind)
                to_prev[groups] = pltpu.roll(out[0], LANES - 64, 1).astype(kind)
                to_next[groups] = pltpu.roll(out[0], LANES - 64 - cy, 1).astype(kind)
            else:
                tail = rows_of((exp, LANES), ex, [*thirds(total[0:1]), *thirds(total[1:2])])[None]
                row = iota((1, exp, 1), 1) >= ex
                to_next[0:groups] = jnp.where(row, tail, nxt).astype(kind)
                to_prev[0:groups] = jnp.where(row, tail, prv).astype(kind)

        shapes = [sds(full_q, F32)] + [sds((groups + first, exp, LANES), kind)] * 2 + ([] if first else [small])
        ins = (1 if first else levels + 1) + n_strips
        return call(body, "lon_first" if first else "lon_last" if last else "lon", ins, shapes)

    far = list(range(2, n_lat - 1))

    def gathered(ix, q, from_prev, from_next, p, last):
        width = HALO if last else PACK
        groups, _ = packing(width)
        has_lo, has_hi = masks(ix, 2, n_lat)
        lane = iota((1, 1, LANES), 2)
        mine = q[p * groups : (p + 1) * groups]
        from_prev, from_next = from_prev[0:groups], from_next[0:groups]

        def put(total, packed, start, here, wide, where):
            ok = (lane >= start) & (lane < start + wide) & (here > 0)
            return total + jnp.where(ok, pltpu.roll(packed, (start - where) % LANES, 2), 0.0)

        at = p * width
        if last:
            mine = put(mine, from_prev, HALO, has_lo, HALO, at)
            return put(mine, from_next, cy, has_hi, HALO, at)
        mine = put(mine, from_prev, 0, has_lo, STRIP, at)
        mine = put(mine, from_prev, 0, has_lo, HALO, at + STRIP)
        mine = put(mine, from_next, cy, has_hi, STRIP, at)
        return put(mine, from_next, cy + HALO, has_hi, HALO, at + STRIP)

    def own_cells():
        row, lane = iota((exp, LANES), 0), iota((exp, LANES), 1)
        inside = (row >= HALO) & (row < HALO + cx) & (lane >= HALO) & (lane < HALO + cy)
        return inside.astype(F32)

    def start_body(ix, q, r_prev, r_next, g_out, keep_out, gg):
        groups, packs = packing(PACK)
        from_prev, from_next = r_prev[...].astype(F32), r_next[...].astype(F32)
        has_lo, has_hi = masks(ix, 2, n_lat)
        lane = iota((exp, LANES), 1)
        row = iota((exp, LANES), 0)
        mine = pltpu.roll(q[0], LANES - 64, 1)
        lo = from_prev[groups]
        hi = pltpu.roll(from_next[groups], cy, 1)
        keep = jnp.where(lane < ey, mine, 0.0)
        keep = keep + jnp.where((lane < STRIP) & (has_lo > 0), lo, 0.0)
        keep = keep + jnp.where((lane >= cy) & (lane < ey) & (has_hi > 0), hi, 0.0)
        keep = jnp.where(row < ex, keep, 0.0)
        keep_out[...] = keep
        acc = jnp.zeros((exp, LANES), F32)
        for p in range(packs):
            g = -(keep[None] * gathered(ix, q, from_prev, from_next, p, False))
            g_out[p * groups : (p + 1) * groups] = g
            acc = acc + jnp.sum(g * g, axis=0)
        gg[...] = jnp.broadcast_to(jnp.sum(acc * own_cells()), (8, LANES))

    g_shape = sds(full_q, F32)
    start_step = call(start_body, "start_step", 3, [g_shape, sds((exp, LANES), F32), small])
    final_shape = sds((members, levels, cx, cy), F32)

    def step(first, last):
        groups, packs = packing(HALO if last else PACK)

        def body(ix, q, r_prev, r_next, sums, keep, g, *rest):
            tiny, rest = rest[: len(far)], rest[len(far) :]
            if not first:
                c_in, rest = rest[0], rest[1:]
            g_out, c_out = rest[:2]
            from_prev, from_next = r_prev[...].astype(F32), r_next[...].astype(F32)
            total = sums[...]
            for ref in tiny:
                total = total + ref[...]
            gg, dot = total[0:1], total[1:2]
            for ref in [r_prev, r_next] if n_lat > 2 else [r_next] if n_lat == 2 else []:
                more = tail_sums(ref[0], ex)
                gg, dot = gg + more[0], dot + more[1]
            alpha = (gg / (gg + dot))[None]
            kept = keep[...][None]
            acc = jnp.zeros((exp, LANES), F32)
            for p in range(packs):
                at = slice(p * groups, (p + 1) * groups)
                old = g[at]
                image = old + kept * gathered(ix, q, from_prev, from_next, p, last)
                new = old - alpha * image
                ctl = -alpha * old if first else c_in[at] - alpha * old
                if not last:
                    g_out[at] = new
                    c_out[at] = ctl
                    acc = acc + jnp.sum(new * new, axis=0)
                else:
                    for ref, val in ((g_out, new), (c_out, ctl)):
                        val = pltpu.roll(pltpu.roll(val, LANES - HALO, 2), exp - HALO, 1)
                        for i in range(groups):
                            f = p * groups + i
                            ref[f % members, level(f // members, ix)] = val[i, :cx, :cy]
            if not last:
                rest[2][...] = jnp.broadcast_to(jnp.sum(acc * own_cells()), (8, LANES))

        shapes = [final_shape] * 2 if last else [g_shape, g_shape, small]
        return call(body, "last_step" if last else "step", 6 + len(far) + (not first), shapes)

    def ring(size, d):
        return [(i, (i + d) % size) for i in range(size)]

    def exchange(qs, strips, sc, ix, first, last):
        if n_lon == 2:
            recv = [lax.ppermute(strips[0], "lon", ring(2, 1))]
        else:
            recv = [lax.ppermute(strips[0], "lon", ring(n_lon, 1)), lax.ppermute(strips[1], "lon", ring(n_lon, -1))]
        out, to_next, to_prev, *sums = lon_join(first, last)(ix, *qs, *sc, *recv)
        if not first and n_lon > 2:
            for d in range(2, n_lon - 1):
                sums[0] = sums[0] + lax.ppermute(sc[0], "lon", ring(n_lon, d))
        from_prev = lax.ppermute(to_next, "lat", ring(n_lat, 1))
        from_next = lax.ppermute(to_prev, "lat", ring(n_lat, -1))
        tiny = [] if first else [lax.ppermute(sums[0], "lat", ring(n_lat, d)) for d in far]
        return out, from_prev, from_next, sums, tiny

    def local(ensemble, huber, innovation, sea_mask):
        slot = lax.broadcasted_iota(jnp.int32, (3,), 0)
        ix = jnp.where(
            slot == 0,
            lax.axis_index("mem"),
            jnp.where(slot == 1, lax.axis_index("lon"), lax.axis_index("lat")),
        ).astype(jnp.int32)
        extra = jnp.pad(
            sea_mask.astype(F32),
            ((HALO, exp - HALO - cx), (64 + HALO, LANES - 64 - HALO - cy)),
        )
        far_off = [pltpu.with_memory_space_constraint(x, pltpu.HBM) for x in (ensemble, huber, innovation, at_tab, bn_tab)]
        q, *strips = first_adjoint(ix, *far_off, extra)
        q, r_prev, r_next, _, _ = exchange([q], strips, [], ix, True, False)
        g, keep, gg = start_step(ix, q, r_prev, r_next)
        control = []
        sends = sorted(range(1, n_mem), key=lambda d: (-min(d, n_mem - d), d))
        for it in range(ITERS):
            last = it == ITERS - 1
            parts = {d: forward(d)(ix, ensemble, g, keep, a_tab, bt_tab, gg)[0] for d in sends + [0]}
            moved = {d: lax.ppermute(parts[d], "mem", ring(n_mem, d)) for d in sends}
            mis, ggm = misfit_own(ix, huber, parts[0], *[moved[d] for d in sends])
            every = {d: lax.ppermute(mis, "mem", ring(n_mem, -d)) for d in sends}
            every[0] = mis
            qs, dots = [], []
            for d in order[:-1]:
                q, dot = adjoint(d, 0)(ix, ensemble, huber, at_tab, bn_tab, every[d])
                qs.append(q)
                dots.append(dot)
            d = order[-1]
            q, sc, *strips = adjoint(d, levels - 1)(
                ix, ensemble, huber, at_tab, bn_tab, every[d], ggm, *qs, *dots
            )
            by_level = dict(zip(order, qs + [q]))
            q, r_prev, r_next, sums, tiny = exchange(
                [by_level[d] for d in range(levels)], strips, [sc], ix, False, last
            )
            out = step(it == 0, last)(ix, q, r_prev, r_next, *sums, keep, g, *tiny, *control)
            if last:
                return out[1], out[0]
            g, control, gg = out[0], [out[1]], out[2]

    return local


def solution(mesh):
    placed = (
        P("mem", None, None, "lon", "lat"),
        P(None, None, "lon", "lat"),
        P(None, None, "lon", "lat"),
        P("lon", "lat"),
    )

    def local(ensemble, huber, innovation, sea_mask):
        return build(dict(mesh.shape), ensemble.shape, sea_mask.shape)(ensemble, huber, innovation, sea_mask)

    return jax.shard_map(
        local,
        mesh=mesh,
        in_specs=placed,
        out_specs=(P("mem", None, "lon", "lat"), P("mem", None, "lon", "lat")),
        check_vma=False,
    )
```

time: 674 us -> 137 us (0.20); the launches traced: 666 us -> 136 us
  waiting for transfers between devices: 182 us -> 34.2 us
  blocking collectives: 119 us -> 0 us
  local copies, waits for them, and re-layouts: 113 us -> 0.11 us
  other arithmetic: 76.6 us -> 0.7 us
  matrix products: 61.5 us -> 0 us
  Pallas kernels: 0 us -> 58.4 us
  starting transfers between devices: 94.1 us -> 41.8 us
  between operations: 20 us -> 1.05 us
    psum x3 -> x0, blocking collectives: 119 us -> none  [local(): lax.psum((jnp.sum(gradient * gradient), jnp.sum(gradient * image)), ('lon...]
    psum x3 -> x0, waiting for transfers between devices: 112 us -> none  [local(): total = lax.psum(partial_sum, 'mem')]
    dot_general x14 -> x0, matrix products: 61.5 us -> none  [the longest x8 49.3 us: adjoint(): jnp.einsum('xc,mlxy,yd->mlcd', back_x, padded, back_y, precision=lax.Prec...]
    pallas_call x0 -> x36, Pallas kernels: none -> 58.4 us  [the longest x12 17.6 us: local(): forward(d)(ix, ensemble, g, keep, a_tab, bt_tab, gg)[0]]
    ppermute x44 -> x33, starting transfers between devices: 93.4 us -> 41.8 us  [the longest x9 15.2 us: local(): moved = {d: lax.ppermute(parts[d], 'mem', ring(n_mem, d)) for d in sends}]
    slice x52 -> x0, local copies, waits for them, and re-layouts: 41.5 us -> none  [the longest x29 34.3 us: extended(): lax.slice_in_dim(cells, cells.shape[dim] - width, cells.shape[dim], axis=...]
    ppermute x44 -> x33, waiting for transfers between devices: 69.8 us -> 34.2 us  [the longest x3 8.29 us: exchange(): lax.ppermute(sums[0], 'lat', ring(n_lat, d))]
    unnamed x142 -> x14, local copies, waits for them, and re-layouts: 31.1 us -> 0.03 us
  transfers between devices with their start and end apart: 47 -> 33, of which waited for: 31 -> 18; matrix products, arithmetic and copies ran while one was open for 6% -> 0% of each run, Pallas kernels for 0% -> 13%
where the time goes in v1:
time: 137 us; the launch traced here: 136 us
  Pallas kernels  58.4 us (43%)
  starting transfers between devices  41.8 us (31%)
  waiting for transfers between devices  34.2 us (25%)
    pallas_call x12, Pallas kernels, local(): forward(d)(ix, ensemble, g, keep, a_tab, bt_tab, gg)[0]  17.6 us
    ppermute x9, starting transfers between devices, local(): moved = {d: lax.ppermute(parts[d], 'mem', ring(n_mem, d)) for d in sends}  15.2 us
    pallas_call x9, Pallas kernels, local(): q, dot = adjoint(d, 0)(ix, ensemble, huber, at_tab, bn_tab, every[d])  13.8 us
    ppermute x9, starting transfers between devices, local(): every = {d: lax.ppermute(mis, 'mem', ring(n_mem, -d)) for d in sends}  10.4 us
    ppermute x3, waiting for transfers between devices, exchange(): lax.ppermute(sums[0], 'lat', ring(n_lat, d))  8.29 us
    ppermute x4, waiting for transfers between devices, exchange(): recv = [lax.ppermute(strips[0], 'lon', ring(2, 1))]  7.98 us
    ppermute x4, starting transfers between devices, exchange(): from_prev = lax.ppermute(to_next, 'lat', ring(n_lat, 1))  7.64 us
    pallas_call x3, Pallas kernels, local(): step(it == 0, last)(ix, q, r_prev, r_next, *sums, keep, g, *tiny, *control)  7.08 us
  transfers between devices with their start and end apart: 33, of which 18 were waited for; matrix products, arithmetic and copies ran while one was open for 0% of the time, Pallas kernels for 13%

profile of v1, /device:TPU:0, one launch (start us, length us, event | category | flops | bytes accessed | tf_op | source)
XLA Modules:
  0.0 136.3 jit_solution(5855039396507075743)
XLA Ops:
  1.4 6.6 %first_adjoint.1 = (f32[4,20,32,128]{3,2,1,0:T(8,128)S(1)}, f32[80,16,128]{2,1,0:T(8,128)S(1)}) custom-call(s32[3]{0:T(128)S(1)} %compare_select_fusion.1.ix, bf16[20,4,4,64,128]{4,3,2,1,0:T(8,128)(2,1)} %ens.49, f32[4,4,64,128]{3,2,1,0:T(8,128)} %huber.31, f32[4,4,64,128]{3,2,1,0:T(8,128)} %innov.1, bf16[2,160,128]{2,1,0:T(8,128)(2,1)} %constant.29.clone.at, ...), custom_call_target="tpu_custom_call" | custom-call | tf_op jit(solution)/shard_map/first_adjoint/pallas_call | solution.py:476
  8.6 1.7 %collective-permute-done.rest_1_ = f32[80,16,128]{2,1,0:T(8,128)S(1)} collective-permute-done((f32[80,16,128]{2,1,0:T(8,128)S(1)}, f32[80,16,128]{2,1,0:T(8,128)S(1)}, u32[]{:S(2)}, u32[]{:S(2)}) %collective-permute-start) | collective-permute-done | bytes 655392 | tf_op jit(solution)/shard_map/ppermute | solution.py:452
  11.7 2.9 %collective-permute-start.1 = (bf16[11,32,128]{2,1,0:T(8,128)(2,1)S(1)}, bf16[11,32,128]{2,1,0:T(8,128)(2,1)S(1)}, u32[]{:S(2)}, u32[]{:S(2)}) collective-permute-start(bf16[11,32,128]{2,1,0:T(8,128)(2,1)S(1)} %get-tuple-element.66), channel_id=1, source_target_pairs={{0,4},{4,8},{8,12},{12,0},{1,5},{5,9},{9,13},{13,1},{2,6},{6,10},{... | collective-permute-start | bytes 270344 | tf_op jit(solution)/shard_map/ppermute | solution.py:459
  15.6 3.3 %collective-permute-done.1.r_prev = bf16[11,32,128]{2,1,0:T(8,128)(2,1)S(1)} collective-permute-done((bf16[11,32,128]{2,1,0:T(8,128)(2,1)S(1)}, bf16[11,32,128]{2,1,0:T(8,128)(2,1)S(1)}, u32[]{:S(2)}, u32[]{:S(2)}) %collective-permute-start.1) | collective-permute-done | bytes 90144 | tf_op jit(solution)/shard_map/ppermute | solution.py:459
  18.9 1.7 %collective-permute-done.2.r_next = bf16[11,32,128]{2,1,0:T(8,128)(2,1)S(1)} collective-permute-done((bf16[11,32,128]{2,1,0:T(8,128)(2,1)S(1)}, bf16[11,32,128]{2,1,0:T(8,128)(2,1)S(1)}, u32[]{:S(2)}, u32[]{:S(2)}) %collective-permute-start.2) | collective-permute-done | bytes 90144 | tf_op jit(solution)/shard_map/ppermute | solution.py:460
  26.7 2.6 %collective-permute-start.3 = (bf16[272,128]{1,0:T(8,128)(2,1)S(1)}, bf16[272,128]{1,0:T(8,128)(2,1)S(1)}, u32[]{:S(2)}, u32[]{:S(2)}) collective-permute-start(bf16[272,128]{1,0:T(8,128)(2,1)S(1)} %forward2.3), channel_id=1, source_target_pairs={{0,2},{1,3},{2,0},{3,1},{4,6},{5,7},{6,4},{7,5},{8,10},{9,11},{10,... | collective-permute-start | bytes 208904 | tf_op jit(solution)/shard_map/ppermute | solution.py:484
  30.9 2.2 %collective-permute-start.5 = (bf16[272,128]{1,0:T(8,128)(2,1)S(1)}, bf16[272,128]{1,0:T(8,128)(2,1)S(1)}, u32[]{:S(2)}, u32[]{:S(2)}) collective-permute-start(bf16[272,128]{1,0:T(8,128)(2,1)S(1)} %forward3.3), channel_id=1, source_target_pairs={{0,3},{1,0},{2,1},{3,2},{4,7},{5,4},{6,5},{7,6},{8,11},{9,8},{10,9... | collective-permute-start | bytes 208904 | tf_op jit(solution)/shard_map/ppermute | solution.py:484
  36.5 3.4 %collective-permute-start.6 = (bf16[256,128]{1,0:T(8,128)(2,1)S(1)}, bf16[256,128]{1,0:T(8,128)(2,1)S(1)}, u32[]{:S(2)}, u32[]{:S(2)}) collective-permute-start(bf16[256,128]{1,0:T(8,128)(2,1)S(1)} %get-tuple-element.71.mis), channel_id=1, source_target_pairs={{0,3},{1,0},{2,1},{3,2},{4,7},{5,4},{6,5},{7,6},{8,11},{9,8},{10,9... | collective-permute-start | bytes 196616 | tf_op jit(solution)/shard_map/ppermute | solution.py:486
  43.6 2.3 %collective-permute-done.8.mis = bf16[256,128]{1,0:T(8,128)(2,1)S(1)} collective-permute-done((bf16[256,128]{1,0:T(8,128)(2,1)S(1)}, bf16[256,128]{1,0:T(8,128)(2,1)S(1)}, u32[]{:S(2)}, u32[]{:S(2)}) %collective-permute-start.8) | collective-permute-done | bytes 65568 | tf_op jit(solution)/shard_map/ppermute | solution.py:486
  49.1 2.1 %collective-permute-done.9.rest_5_ = f32[80,16,128]{2,1,0:T(8,128)S(1)} collective-permute-done((f32[80,16,128]{2,1,0:T(8,128)S(1)}, f32[80,16,128]{2,1,0:T(8,128)S(1)}, u32[]{:S(2)}, u32[]{:S(2)}) %collective-permute-start.9) | collective-permute-done | bytes 655392 | tf_op jit(solution)/shard_map/ppermute | solution.py:452
  56.1 3.1 %collective-permute-done.12.rest_0_ = f32[8,128]{1,0:T(8,128)S(1)} collective-permute-done((f32[8,128]{1,0:T(8,128)S(1)}, f32[8,128]{1,0:T(8,128)S(1)}, u32[]{:S(2)}, u32[]{:S(2)}) %collective-permute-start.12) | collective-permute-done | bytes 4128 | tf_op jit(solution)/shard_map/ppermute | solution.py:461
  65.4 2.2 %collective-permute-start.14 = (bf16[272,128]{1,0:T(8,128)(2,1)S(1)}, bf16[272,128]{1,0:T(8,128)(2,1)S(1)}, u32[]{:S(2)}, u32[]{:S(2)}) collective-permute-start(bf16[272,128]{1,0:T(8,128)(2,1)S(1)} %forward1.4), channel_id=1, source_target_pairs={{0,1},{1,2},{2,3},{3,0},{4,5},{5,6},{6,7},{7,4},{8,9},{9,10},{10,1... | collective-permute-start | bytes 208904 | tf_op jit(solution)/shard_map/ppermute | solution.py:484
  70.7 2.6 %collective-permute-done.13.rest_1_ = bf16[272,128]{1,0:T(8,128)(2,1)S(1)} collective-permute-done((bf16[272,128]{1,0:T(8,128)(2,1)S(1)}, bf16[272,128]{1,0:T(8,128)(2,1)S(1)}, u32[]{:S(2)}, u32[]{:S(2)}) %collective-permute-start.13) | collective-permute-done | bytes 69664 | tf_op jit(solution)/shard_map/ppermute | solution.py:484
  73.9 2.1 %collective-permute-start.16 = (bf16[256,128]{1,0:T(8,128)(2,1)S(1)}, bf16[256,128]{1,0:T(8,128)(2,1)S(1)}, u32[]{:S(2)}, u32[]{:S(2)}) collective-permute-start(bf16[256,128]{1,0:T(8,128)(2,1)S(1)} %get-tuple-element.88.mis), channel_id=1, source_target_pairs={{0,3},{1,0},{2,1},{3,2},{4,7},{5,4},{6,5},{7,6},{8,11},{9,8},{10,9... | collective-permute-start | bytes 196616 | tf_op jit(solution)/shard_map/ppermute | solution.py:486
  85.2 2.1 %collective-permute-done.19.rest_5_ = f32[80,16,128]{2,1,0:T(8,128)S(1)} collective-permute-done((f32[80,16,128]{2,1,0:T(8,128)S(1)}, f32[80,16,128]{2,1,0:T(8,128)S(1)}, u32[]{:S(2)}, u32[]{:S(2)}) %collective-permute-start.19) | collective-permute-done | bytes 655392 | tf_op jit(solution)/shard_map/ppermute | solution.py:452
  92.9 2.4 %collective-permute-done.22.rest_0_ = f32[8,128]{1,0:T(8,128)S(1)} collective-permute-done((f32[8,128]{1,0:T(8,128)S(1)}, f32[8,128]{1,0:T(8,128)S(1)}, u32[]{:S(2)}, u32[]{:S(2)}) %collective-permute-start.22) | collective-permute-done | bytes 4128 | tf_op jit(solution)/shard_map/ppermute | solution.py:461
  104.0 2.5 %collective-permute-start.25 = (bf16[272,128]{1,0:T(8,128)(2,1)S(1)}, bf16[272,128]{1,0:T(8,128)(2,1)S(1)}, u32[]{:S(2)}, u32[]{:S(2)}) collective-permute-start(bf16[272,128]{1,0:T(8,128)(2,1)S(1)} %forward3.5), channel_id=1, source_target_pairs={{0,3},{1,0},{2,1},{3,2},{4,7},{5,4},{6,5},{7,6},{8,11},{9,8},{10,9... | collective-permute-start | bytes 208904 | tf_op jit(solution)/shard_map/ppermute | solution.py:484
  108.0 1.9 %collective-permute-done.23.rest_1_ = bf16[272,128]{1,0:T(8,128)(2,1)S(1)} collective-permute-done((bf16[272,128]{1,0:T(8,128)(2,1)S(1)}, bf16[272,128]{1,0:T(8,128)(2,1)S(1)}, u32[]{:S(2)}, u32[]{:S(2)}) %collective-permute-start.23) | collective-permute-done | bytes 69664 | tf_op jit(solution)/shard_map/ppermute | solution.py:484
  110.5 2.8 %collective-permute-start.26 = (bf16[256,128]{1,0:T(8,128)(2,1)S(1)}, bf16[256,128]{1,0:T(8,128)(2,1)S(1)}, u32[]{:S(2)}, u32[]{:S(2)}) collective-permute-start(bf16[256,128]{1,0:T(8,128)(2,1)S(1)} %get-tuple-element.106.mis), channel_id=1, source_target_pairs={{0,3},{1,0},{2,1},{3,2},{4,7},{5,4},{6,5},{7,6},{8,11},{9,8},{10,9... | collective-permute-start | bytes 196616 | tf_op jit(solution)/shard_map/ppermute | solution.py:486
  117.2 2.1 %collective-permute-done.28.mis = bf16[256,128]{1,0:T(8,128)(2,1)S(1)} collective-permute-done((bf16[256,128]{1,0:T(8,128)(2,1)S(1)}, bf16[256,128]{1,0:T(8,128)(2,1)S(1)}, u32[]{:S(2)}, u32[]{:S(2)}) %collective-permute-start.28) | collective-permute-done | bytes 65568 | tf_op jit(solution)/shard_map/ppermute | solution.py:486
  122.6 2.1 %collective-permute-done.29.rest_5_ = f32[80,16,128]{2,1,0:T(8,128)S(1)} collective-permute-done((f32[80,16,128]{2,1,0:T(8,128)S(1)}, f32[80,16,128]{2,1,0:T(8,128)S(1)}, u32[]{:S(2)}, u32[]{:S(2)}) %collective-permute-start.29) | collective-permute-done | bytes 655392 | tf_op jit(solution)/shard_map/ppermute | solution.py:452
  126.0 1.8 %collective-permute-start.30 = (f32[4,32,128]{2,1,0:T(8,128)S(1)}, f32[4,32,128]{2,1,0:T(8,128)S(1)}, u32[]{:S(2)}, u32[]{:S(2)}) collective-permute-start(f32[4,32,128]{2,1,0:T(8,128)S(1)} %get-tuple-element.118), channel_id=1, source_target_pairs={{0,4},{4,8},{8,12},{12,0},{1,5},{5,9},{9,13},{13,1},{2,6},{6,10},{... | collective-permute-start | bytes 196616 | tf_op jit(solution)/shard_map/ppermute | solution.py:459
  129.8 2.7 %collective-permute-done.32.rest_0_ = f32[8,128]{1,0:T(8,128)S(1)} collective-permute-done((f32[8,128]{1,0:T(8,128)S(1)}, f32[8,128]{1,0:T(8,128)S(1)}, u32[]{:S(2)}, u32[]{:S(2)}) %collective-permute-start.32) | collective-permute-done | bytes 4128 | tf_op jit(solution)/shard_map/ppermute | solution.py:461
  132.6 3.8 %last_step.1 = (f32[20,4,16,32]{3,2,1,0:T(8,128)}, f32[20,4,16,32]{3,2,1,0:T(8,128)}) custom-call(s32[3]{0:T(128)S(1)} %compare_select_fusion.1.ix, f32[80,32,128]{2,1,0:T(8,128)S(1)} %get-tuple-element.117.q, f32[4,32,128]{2,1,0:T(8,128)S(1)} %collective-permute-done.30.r_prev, f32[4,32,128]{2,1,0:T(8,128)S(1)} %collective-permute-done.31.r_next, ...), custom_call_target="tpu_custom_call" | custom-call | tf_op jit(solution)/shard_map/last_step/pallas_call | solution.py:501
  (96 shorter events, 72.1 us)
Async XLA Ops:
  11.7 7.2 %collective-permute-start.1 = (bf16[11,32,128]{2,1,0:T(8,128)(2,1)S(1)}, bf16[11,32,128]{2,1,0:T(8,128)(2,1)S(1)}, u32[]{:S(2)}, u32[]{:S(2)}) collective-permute-start(bf16[11,32,128]{2,1,0:T(8,128)(2,1)S(1)} %get-tuple-element.66), channel_id=1, source_target_pairs={{0,4},{4,8},{8,12},{12,0},{1,5},{5,9},{9,13},{13,1},{2,6},{6,10},{... | collective-permute-start | bytes 270344 | tf_op jit(solution)/shard_map/ppermute | solution.py:459
  14.6 6.1 %collective-permute-start.2 = (bf16[11,32,128]{2,1,0:T(8,128)(2,1)S(1)}, bf16[11,32,128]{2,1,0:T(8,128)(2,1)S(1)}, u32[]{:S(2)}, u32[]{:S(2)}) collective-permute-start(bf16[11,32,128]{2,1,0:T(8,128)(2,1)S(1)} %get-tuple-element.67), channel_id=1, source_target_pairs={{0,12},{4,0},{8,4},{12,8},{1,13},{5,1},{9,5},{13,9},{2,14},{6,2},{... | collective-permute-start | bytes 270344 | tf_op jit(solution)/shard_map/ppermute | solution.py:460
  26.7 7.9 %collective-permute-start.3 = (bf16[272,128]{1,0:T(8,128)(2,1)S(1)}, bf16[272,128]{1,0:T(8,128)(2,1)S(1)}, u32[]{:S(2)}, u32[]{:S(2)}) collective-permute-start(bf16[272,128]{1,0:T(8,128)(2,1)S(1)} %forward2.3), channel_id=1, source_target_pairs={{0,2},{1,3},{2,0},{3,1},{4,6},{5,7},{6,4},{7,5},{8,10},{9,11},{10,... | collective-permute-start | bytes 208904 | tf_op jit(solution)/shard_map/ppermute | solution.py:484
  29.3 6.2 %collective-permute-start.4 = (bf16[272,128]{1,0:T(8,128)(2,1)S(1)}, bf16[272,128]{1,0:T(8,128)(2,1)S(1)}, u32[]{:S(2)}, u32[]{:S(2)}) collective-permute-start(bf16[272,128]{1,0:T(8,128)(2,1)S(1)} %forward1.3), channel_id=1, source_target_pairs={{0,1},{1,2},{2,3},{3,0},{4,5},{5,6},{6,7},{7,4},{8,9},{9,10},{10,1... | collective-permute-start | bytes 208904 | tf_op jit(solution)/shard_map/ppermute | solution.py:484
  30.9 5.1 %collective-permute-start.5 = (bf16[272,128]{1,0:T(8,128)(2,1)S(1)}, bf16[272,128]{1,0:T(8,128)(2,1)S(1)}, u32[]{:S(2)}, u32[]{:S(2)}) collective-permute-start(bf16[272,128]{1,0:T(8,128)(2,1)S(1)} %forward3.3), channel_id=1, source_target_pairs={{0,3},{1,0},{2,1},{3,2},{4,7},{5,4},{6,5},{7,6},{8,11},{9,8},{10,9... | collective-permute-start | bytes 208904 | tf_op jit(solution)/shard_map/ppermute | solution.py:484
  36.5 5.5 %collective-permute-start.6 = (bf16[256,128]{1,0:T(8,128)(2,1)S(1)}, bf16[256,128]{1,0:T(8,128)(2,1)S(1)}, u32[]{:S(2)}, u32[]{:S(2)}) collective-permute-start(bf16[256,128]{1,0:T(8,128)(2,1)S(1)} %get-tuple-element.71.mis), channel_id=1, source_target_pairs={{0,3},{1,0},{2,1},{3,2},{4,7},{5,4},{6,5},{7,6},{8,11},{9,8},{10,9... | collective-permute-start | bytes 196616 | tf_op jit(solution)/shard_map/ppermute | solution.py:486
  39.9 6.1 %collective-permute-start.8 = (bf16[256,128]{1,0:T(8,128)(2,1)S(1)}, bf16[256,128]{1,0:T(8,128)(2,1)S(1)}, u32[]{:S(2)}, u32[]{:S(2)}) collective-permute-start(bf16[256,128]{1,0:T(8,128)(2,1)S(1)} %get-tuple-element.71.mis), channel_id=1, source_target_pairs={{0,1},{1,2},{2,3},{3,0},{4,5},{5,6},{6,7},{7,4},{8,9},{9,10},{10,1... | collective-permute-start | bytes 196616 | tf_op jit(solution)/shard_map/ppermute | solution.py:486
  39.9 7.6 %collective-permute-start.7 = (bf16[256,128]{1,0:T(8,128)(2,1)S(1)}, bf16[256,128]{1,0:T(8,128)(2,1)S(1)}, u32[]{:S(2)}, u32[]{:S(2)}) collective-permute-start(bf16[256,128]{1,0:T(8,128)(2,1)S(1)} %get-tuple-element.71.mis), channel_id=1, source_target_pairs={{0,2},{1,3},{2,0},{3,1},{4,6},{5,7},{6,4},{7,5},{8,10},{9,11},{10,... | collective-permute-start | bytes 196616 | tf_op jit(solution)/shard_map/ppermute | solution.py:486
  52.6 6.6 %collective-permute-start.10 = (bf16[10,32,128]{2,1,0:T(8,128)(2,1)S(1)}, bf16[10,32,128]{2,1,0:T(8,128)(2,1)S(1)}, u32[]{:S(2)}, u32[]{:S(2)}) collective-permute-start(bf16[10,32,128]{2,1,0:T(8,128)(2,1)S(1)} %get-tuple-element.83), channel_id=1, source_target_pairs={{0,4},{4,8},{8,12},{12,0},{1,5},{5,9},{9,13},{13,1},{2,6},{6,10},{... | collective-permute-start | bytes 245768 | tf_op jit(solution)/shard_map/ppermute | solution.py:459
  65.3 8.0 %collective-permute-start.13 = (bf16[272,128]{1,0:T(8,128)(2,1)S(1)}, bf16[272,128]{1,0:T(8,128)(2,1)S(1)}, u32[]{:S(2)}, u32[]{:S(2)}) collective-permute-start(bf16[272,128]{1,0:T(8,128)(2,1)S(1)} %forward2.4), channel_id=1, source_target_pairs={{0,2},{1,3},{2,0},{3,1},{4,6},{5,7},{6,4},{7,5},{8,10},{9,11},{10,... | collective-permute-start | bytes 208904 | tf_op jit(solution)/shard_map/ppermute | solution.py:484
  65.4 7.9 %collective-permute-start.14 = (bf16[272,128]{1,0:T(8,128)(2,1)S(1)}, bf16[272,128]{1,0:T(8,128)(2,1)S(1)}, u32[]{:S(2)}, u32[]{:S(2)}) collective-permute-start(bf16[272,128]{1,0:T(8,128)(2,1)S(1)} %forward1.4), channel_id=1, source_target_pairs={{0,1},{1,2},{2,3},{3,0},{4,5},{5,6},{6,7},{7,4},{8,9},{9,10},{10,1... | collective-permute-start | bytes 208904 | tf_op jit(solution)/shard_map/ppermute | solution.py:484
  67.6 5.7 %collective-permute-start.15 = (bf16[272,128]{1,0:T(8,128)(2,1)S(1)}, bf16[272,128]{1,0:T(8,128)(2,1)S(1)}, u32[]{:S(2)}, u32[]{:S(2)}) collective-permute-start(bf16[272,128]{1,0:T(8,128)(2,1)S(1)} %forward3.4), channel_id=1, source_target_pairs={{0,3},{1,0},{2,1},{3,2},{4,7},{5,4},{6,5},{7,6},{8,11},{9,8},{10,9... | collective-permute-start | bytes 208904 | tf_op jit(solution)/shard_map/ppermute | solution.py:484
  73.9 5.7 %collective-permute-start.16 = (bf16[256,128]{1,0:T(8,128)(2,1)S(1)}, bf16[256,128]{1,0:T(8,128)(2,1)S(1)}, u32[]{:S(2)}, u32[]{:S(2)}) collective-permute-start(bf16[256,128]{1,0:T(8,128)(2,1)S(1)} %get-tuple-element.88.mis), channel_id=1, source_target_pairs={{0,3},{1,0},{2,1},{3,2},{4,7},{5,4},{6,5},{7,6},{8,11},{9,8},{10,9... | collective-permute-start | bytes 196616 | tf_op jit(solution)/shard_map/ppermute | solution.py:486
  76.0 6.1 %collective-permute-start.18 = (bf16[256,128]{1,0:T(8,128)(2,1)S(1)}, bf16[256,128]{1,0:T(8,128)(2,1)S(1)}, u32[]{:S(2)}, u32[]{:S(2)}) collective-permute-start(bf16[256,128]{1,0:T(8,128)(2,1)S(1)} %get-tuple-element.88.mis), channel_id=1, source_target_pairs={{0,1},{1,2},{2,3},{3,0},{4,5},{5,6},{6,7},{7,4},{8,9},{9,10},{10,1... | collective-permute-start | bytes 196616 | tf_op jit(solution)/shard_map/ppermute | solution.py:486
  76.0 7.6 %collective-permute-start.17 = (bf16[256,128]{1,0:T(8,128)(2,1)S(1)}, bf16[256,128]{1,0:T(8,128)(2,1)S(1)}, u32[]{:S(2)}, u32[]{:S(2)}) collective-permute-start(bf16[256,128]{1,0:T(8,128)(2,1)S(1)} %get-tuple-element.88.mis), channel_id=1, source_target_pairs={{0,2},{1,3},{2,0},{3,1},{4,6},{5,7},{6,4},{7,5},{8,10},{9,11},{10,... | collective-permute-start | bytes 196616 | tf_op jit(solution)/shard_map/ppermute | solution.py:486
  88.7 6.6 %collective-permute-start.20 = (bf16[10,32,128]{2,1,0:T(8,128)(2,1)S(1)}, bf16[10,32,128]{2,1,0:T(8,128)(2,1)S(1)}, u32[]{:S(2)}, u32[]{:S(2)}) collective-permute-start(bf16[10,32,128]{2,1,0:T(8,128)(2,1)S(1)} %get-tuple-element.100), channel_id=1, source_target_pairs={{0,4},{4,8},{8,12},{12,0},{1,5},{5,9},{9,13},{13,1},{2,6},{6,10},{... | collective-permute-start | bytes 245768 | tf_op jit(solution)/shard_map/ppermute | solution.py:459
  90.1 5.5 %collective-permute-start.21 = (bf16[10,32,128]{2,1,0:T(8,128)(2,1)S(1)}, bf16[10,32,128]{2,1,0:T(8,128)(2,1)S(1)}, u32[]{:S(2)}, u32[]{:S(2)}) collective-permute-start(bf16[10,32,128]{2,1,0:T(8,128)(2,1)S(1)} %get-tuple-element.101), channel_id=1, source_target_pairs={{0,12},{4,0},{8,4},{12,8},{1,13},{5,1},{9,5},{13,9},{2,14},{6,2},{... | collective-permute-start | bytes 245768 | tf_op jit(solution)/shard_map/ppermute | solution.py:460
  101.7 8.2 %collective-permute-start.23 = (bf16[272,128]{1,0:T(8,128)(2,1)S(1)}, bf16[272,128]{1,0:T(8,128)(2,1)S(1)}, u32[]{:S(2)}, u32[]{:S(2)}) collective-permute-start(bf16[272,128]{1,0:T(8,128)(2,1)S(1)} %forward2.5), channel_id=1, source_target_pairs={{0,2},{1,3},{2,0},{3,1},{4,6},{5,7},{6,4},{7,5},{8,10},{9,11},{10,... | collective-permute-start | bytes 208904 | tf_op jit(solution)/shard_map/ppermute | solution.py:484
  102.7 7.2 %collective-permute-start.24 = (bf16[272,128]{1,0:T(8,128)(2,1)S(1)}, bf16[272,128]{1,0:T(8,128)(2,1)S(1)}, u32[]{:S(2)}, u32[]{:S(2)}) collective-permute-start(bf16[272,128]{1,0:T(8,128)(2,1)S(1)} %forward1.5), channel_id=1, source_target_pairs={{0,1},{1,2},{2,3},{3,0},{4,5},{5,6},{6,7},{7,4},{8,9},{9,10},{10,1... | collective-permute-start | bytes 208904 | tf_op jit(solution)/shard_map/ppermute | solution.py:484
  104.0 5.9 %collective-permute-start.25 = (bf16[272,128]{1,0:T(8,128)(2,1)S(1)}, bf16[272,128]{1,0:T(8,128)(2,1)S(1)}, u32[]{:S(2)}, u32[]{:S(2)}) collective-permute-start(bf16[272,128]{1,0:T(8,128)(2,1)S(1)} %forward3.5), channel_id=1, source_target_pairs={{0,3},{1,0},{2,1},{3,2},{4,7},{5,4},{6,5},{7,6},{8,11},{9,8},{10,9... | collective-permute-start | bytes 208904 | tf_op jit(solution)/shard_map/ppermute | solution.py:484
  110.5 5.2 %collective-permute-start.26 = (bf16[256,128]{1,0:T(8,128)(2,1)S(1)}, bf16[256,128]{1,0:T(8,128)(2,1)S(1)}, u32[]{:S(2)}, u32[]{:S(2)}) collective-permute-start(bf16[256,128]{1,0:T(8,128)(2,1)S(1)} %get-tuple-element.106.mis), channel_id=1, source_target_pairs={{0,3},{1,0},{2,1},{3,2},{4,7},{5,4},{6,5},{7,6},{8,11},{9,8},{10,9... | collective-permute-start | bytes 196616 | tf_op jit(solution)/shard_map/ppermute | solution.py:486
  113.3 6.1 %collective-permute-start.28 = (bf16[256,128]{1,0:T(8,128)(2,1)S(1)}, bf16[256,128]{1,0:T(8,128)(2,1)S(1)}, u32[]{:S(2)}, u32[]{:S(2)}) collective-permute-start(bf16[256,128]{1,0:T(8,128)(2,1)S(1)} %get-tuple-element.106.mis), channel_id=1, source_target_pairs={{0,1},{1,2},{2,3},{3,0},{4,5},{5,6},{6,7},{7,4},{8,9},{9,10},{10,1... | collective-permute-start | bytes 196616 | tf_op jit(solution)/shard_map/ppermute | solution.py:486
  113.3 7.6 %collective-permute-start.27 = (bf16[256,128]{1,0:T(8,128)(2,1)S(1)}, bf16[256,128]{1,0:T(8,128)(2,1)S(1)}, u32[]{:S(2)}, u32[]{:S(2)}) collective-permute-start(bf16[256,128]{1,0:T(8,128)(2,1)S(1)} %get-tuple-element.106.mis), channel_id=1, source_target_pairs={{0,2},{1,3},{2,0},{3,1},{4,6},{5,7},{6,4},{7,5},{8,10},{9,11},{10,... | collective-permute-start | bytes 196616 | tf_op jit(solution)/shard_map/ppermute | solution.py:486
  126.0 6.6 %collective-permute-start.30 = (f32[4,32,128]{2,1,0:T(8,128)S(1)}, f32[4,32,128]{2,1,0:T(8,128)S(1)}, u32[]{:S(2)}, u32[]{:S(2)}) collective-permute-start(f32[4,32,128]{2,1,0:T(8,128)S(1)} %get-tuple-element.118), channel_id=1, source_target_pairs={{0,4},{4,8},{8,12},{12,0},{1,5},{5,9},{9,13},{13,1},{2,6},{6,10},{... | collective-permute-start | bytes 196616 | tf_op jit(solution)/shard_map/ppermute | solution.py:459
  (16 other events, 131.7 us)
